TPU v7x, 256 devices: a whole 4x4x8 slice. The times are simulated.
256 devices in a mesh: feat: 8 (over y, core), dom: 32 (over z, x).
Axes of the slice: x: 4, y: 4, z: 8, core: 2. Of those that a mesh axis runs over, the one named last changes fastest.
Arguments:
- features: bfloat16 [8, 4096, 4096], P(None, 'dom', 'feat'), may hold values from -6 to 6
- w_one: bfloat16 [4096, 1024], P('feat'), may hold values from -0.09375 to 0.09375
- w_two: bfloat16 [1024, 512], replicated, may hold values from -0.25 to 0.25
- neighbor: int32 [8, 4096, 10], P('feat', 'dom'), may hold values from 0 to 383
- degree: int32 [8, 4096], P('feat', 'dom'), may hold values from 1 to 10
- send_rows: int32 [8, 1024, 8], P('feat', 'dom'), may hold values from 0 to 127
- grad_out: bfloat16 [8, 4096, 512], P('feat', 'dom'), may hold values from -6 to 6
Outputs:
- out_two: bfloat16 [8, 4096, 512], P('feat', 'dom')
- grad_one: float32 [4096, 1024], P('feat')
- grad_two: float32 [1024, 512], replicated
All inputs are finite; a program needn't handle non-finite values.
Results may differ from a plain program's by a relative error of at most 0.015.
Values may be sent and summed in bfloat16 or wider, within the bound.
No kernel may reach another device: no remote copies, remote signals or barrier semaphores. Data moves between devices by JAX's collectives and lax.ppermute only.
A program may use at most 64 MiB of HBM per device.

v0:
```python
import math
import jax
import jax.numpy as jnp
from jax import lax
from jax.sharding import PartitionSpec as P


def trade(buffer):
    return lax.all_to_all(buffer, "dom", split_axis=0, concat_axis=0, tiled=True)


def on_device(features, w_one, w_two, neighbor, degree, send_rows, grad_out):
    groups, nodes, cols = features.shape
    width = w_two.shape[1]
    nbrs = neighbor[0]
    degs = degree[0]
    sends = send_rows[0]
    parts = lax.axis_size("dom")
    fan = nbrs.shape[1]
    slots = jnp.arange(fan, dtype=jnp.int32)
    weight = (slots[None, :] < degs[:, None]).astype(jnp.float32) / degs[:, None].astype(
        jnp.float32
    )
    flat = features.reshape(groups * nodes, cols)

    def spread(values):
        boxes = values[sends]
        recv = trade(boxes)
        table = jnp.concatenate([values, recv.reshape(-1, values.shape[1])], axis=0)
        gathered = table[nbrs]
        return jnp.sum(gathered.astype(jnp.float32) * weight[..., None], axis=1)

    def gather_back(grads):
        span = grads.shape[1]
        terms = (weight[..., None] * grads[:, None, :]).reshape(-1, span)
        table = jnp.zeros((nodes + sends.size, span), jnp.float32).at[nbrs.reshape(-1)].add(terms)
        local = table[:nodes]
        outgoing = table[nodes:].astype(jnp.bfloat16).reshape(parts, sends.shape[1], span)
        returned = trade(outgoing)
        home = (
            jnp.zeros((nodes, span), jnp.float32)
            .at[sends.reshape(-1)]
            .add(returned.reshape(-1, span).astype(jnp.float32))
        )
        return local + home

    rows = flat
    proj = lax.psum_scatter(
        jnp.dot(rows, w_one, preferred_element_type=jnp.float32),
        "feat",
        scatter_dimension=0,
        tiled=True,
    )
    p_self = proj[:, :width]
    p_near = proj[:, width:].astype(jnp.bfloat16)
    pre = p_self + spread(p_near)
    hidden = (pre * jax.nn.sigmoid(pre)).astype(jnp.bfloat16)
    agg = spread(hidden).astype(jnp.bfloat16)
    joined = jnp.concatenate([hidden, agg], axis=-1)
    out = jnp.dot(joined, w_two, preferred_element_type=jnp.float32).astype(jnp.bfloat16)
    grads = grad_out[0]
    two_sum = lax.dot_general(
        joined, grads, (((0,), (0,)), ((), ())), preferred_element_type=jnp.float32
    )
    dcat = lax.dot_general(
        grads, w_two, (((1,), (1,)), ((), ())), preferred_element_type=jnp.float32
    )
    d_hidden = dcat[:, :width] + gather_back(dcat[:, width:])
    sig = jax.nn.sigmoid(pre)
    d_pre = d_hidden * sig * (1.0 + pre * (1.0 - sig))
    d_near = gather_back(d_pre)
    d_proj = jnp.concatenate([d_pre, d_near], axis=-1).astype(jnp.bfloat16)
    rows = flat
    one_sum = lax.dot_general(
        rows,
        lax.all_gather(d_proj, "feat", axis=0, tiled=True),
        (((0,), (0,)), ((), ())),
        preferred_element_type=jnp.float32,
    )
    one_sum = lax.psum(one_sum.astype(jnp.bfloat16), "dom").astype(jnp.float32)
    two_sum = lax.psum(two_sum, ("feat", "dom"))
    scale = 1.0 / math.sqrt(groups * nodes * parts)
    return (out[None], one_sum * scale, two_sum * scale)


def solution(mesh):
    in_specs = (
        P(None, "dom", "feat"),
        P("feat", None),
        P(),
        P("feat", "dom", None),
        P("feat", "dom"),
        P("feat", "dom", None),
        P("feat", "dom", None),
    )
    out_specs = (P("feat", "dom", None), P("feat", None), P())
    return jax.shard_map(
        on_device, mesh=mesh, in_specs=in_specs, out_specs=out_specs, check_vma=False
    )
```

profile of v0, /device:TPU:8, one launch (start us, length us, event | category | flops | bytes accessed | tf_op | source)
XLA Modules:
  0.0 582.7 jit_solution(4482622993260259353)
XLA Ops:
  8.4 4.4 fusion.26
  14.5 2.5 mul.73
  17.0 4.5 mul.74
  21.9 13.1 %scatter_custom_fusion = f32[384,512]{1,0:T(8,128)S(1)} fusion(s32[1280]{0:T(1024)S(1)} %fusion.22, f32[1280,512]{1,0:T(8,128)} %mul.74, f32[1280]{0:T(1024)S(1)} %div.23, f32[]{:T(128)} %constant.9.clone.1), kind=kCustom, calls=%fused_computation.12 | custom fusion | flops 1310720 | bytes 3416068 | tf_op jit(solution)/shard_map/scatter-add | solution.py:36
  35.7 11.3 %all-to-all-start.2 = ((bf16[32,8,512]{2,1,0:T(8,128)(2,1)}), bf16[32,8,512]{2,1,0:T(8,128)(2,1)S(1)}, u32[]{:S(2)}, u32[]{:S(2)}) async-start(bf16[32,8,512]{2,1,0:T(8,128)(2,1)} %fusion.14), calls=%async_computation.3 | async-start | bytes 524288 | tf_op jit(solution)/shard_map/all_to_all | solution.py:9
  47.5 5.2 reduce-scatter.2.cloned.1.call-done
  55.5 4.2 all-to-all-done.2
  59.7 5.7 all-to-all-start
  65.6 2.4 scatter_custom_fusion.1
  68.0 10.6 %all-to-all-done = bf16[32,8,512]{2,1,0:T(8,128)(2,1)S(1)} async-done(((bf16[32,8,512]{2,1,0:T(8,128)(2,1)}), bf16[32,8,512]{2,1,0:T(8,128)(2,1)S(1)}, u32[]{:S(2)}, u32[]{:S(2)}) %all-to-all-start) | async-done | bytes 262176 | tf_op jit(solution)/shard_map/all_to_all | solution.py:9
  78.7 4.1 gather_fusion.1
  84.9 3.2 multiply_reduce_fusion.1
  88.3 2.5 mul.79
  90.8 4.5 mul.80
  95.3 13.1 %scatter_custom_fusion.2 = f32[384,512]{1,0:T(8,128)S(1)} fusion(s32[1280]{0:T(1024)S(1)} %fusion.22, f32[1280,512]{1,0:T(8,128)} %mul.80, f32[1280]{0:T(1024)S(1)} %div.23, f32[]{:T(128)} %constant.9.clone.1), kind=kCustom, calls=%fused_computation.10 | custom fusion | flops 1310720 | bytes 3416068 | tf_op jit(solution)/shard_map/scatter-add | solution.py:36
  109.1 3.9 all-to-all-start.3
  113.0 12.2 %all-to-all-done.3 = bf16[32,8,512]{2,1,0:T(8,128)(2,1)S(1)} async-done(((bf16[32,8,512]{2,1,0:T(8,128)(2,1)}), bf16[32,8,512]{2,1,0:T(8,128)(2,1)S(1)}, u32[]{:S(2)}, u32[]{:S(2)}) %all-to-all-start.3) | async-done | bytes 262176 | tf_op jit(solution)/shard_map/all_to_all | solution.py:9
  129.5 15.7 %all_to_all.20 = bf16[32,8,512]{2,1,0:T(8,128)(2,1)S(1)} all-to-all(bf16[32,8,512]{2,1,0:T(8,128)(2,1)S(1)} %bitcast.50), channel_id=1, replica_groups=mesh['feat'=8,'dom'=32] {'dom'}, dimensions={0} | all-to-all | bytes 524288 | tf_op jit(solution)/shard_map/all_to_all | solution.py:9
  145.3 4.1 gather_fusion.3
  151.6 3.2 multiply_reduce_fusion
  156.7 3.9 fusion.4
  161.6 259.2 %all-reduce.5.cloned.1.call-done = f32[1024,512]{1,0:T(8,128)} async-done(((f32[1024,512]{1,0:T(8,128)}), f32[1024,512]{1,0:T(8,128)}) %all-reduce.5.cloned.1.call-update) | async-done | bytes 2097168 | tf_op jit(solution)/shard_map/psum | solution.py:81
  420.8 3.2 broadcast_multiply_fusion
  423.9 148.9 %all-reduce.3.cloned.1.call-done = bf16[512,1024]{0,1:T(8,128)(2,1)} async-done(((bf16[512,1024]{0,1:T(8,128)(2,1)}), bf16[512,1024]{0,1:T(8,128)(2,1)}) %all-reduce.3.cloned.1.call-update) | async-done | bytes 1048592 | tf_op jit(solution)/shard_map/psum | solution.py:80
  (65 shorter events, 23.0 us)
Async XLA Ops:
  7.2 1.2 copy-start
  7.2 45.5 %reduce-scatter.2.cloned.1.call-start = ((), (), s32[]{:S(2)}) async-start(), calls=%async_computation.5 | async-start | bytes 4718592 | tf_op jit(solution)/shard_map/reduce_scatter | solution.py:48
  12.8 0.7 copy-start.6
  12.8 1.2 copy-start.1
  12.8 1.2 copy-start.3
  17.0 4.5 copy-start.8
  21.6 25.4 %copy-start.7 = (s32[1,32,8]{1,2,0:T(8,128)S(1)}, s32[1,32,8]{1,2,0:T(8,128)}, u32[]{:S(2)}) copy-start(s32[1,32,8]{1,2,0:T(8,128)} %param.12) | copy-start | bytes 3076
  35.7 24.0 %all-to-all-start.2 = ((bf16[32,8,512]{2,1,0:T(8,128)(2,1)}), bf16[32,8,512]{2,1,0:T(8,128)(2,1)S(1)}, u32[]{:S(2)}, u32[]{:S(2)}) async-start(bf16[32,8,512]{2,1,0:T(8,128)(2,1)} %fusion.14), calls=%async_computation.3 | async-start | bytes 524288 | tf_op jit(solution)/shard_map/all_to_all | solution.py:9
  59.7 18.9 %all-to-all-start = ((bf16[32,8,512]{2,1,0:T(8,128)(2,1)}), bf16[32,8,512]{2,1,0:T(8,128)(2,1)S(1)}, u32[]{:S(2)}, u32[]{:S(2)}) async-start(bf16[32,8,512]{2,1,0:T(8,128)(2,1)} %bitcast.2), calls=%async_computation.1 | async-start | bytes 524288 | tf_op jit(solution)/shard_map/all_to_all | solution.py:9
  84.9 3.3 copy-start.5
  109.1 16.2 %all-to-all-start.3 = ((bf16[32,8,512]{2,1,0:T(8,128)(2,1)}), bf16[32,8,512]{2,1,0:T(8,128)(2,1)S(1)}, u32[]{:S(2)}, u32[]{:S(2)}) async-start(bf16[32,8,512]{2,1,0:T(8,128)(2,1)} %fusion.15), calls=%async_computation.4 | async-start | bytes 524288 | tf_op jit(solution)/shard_map/all_to_all | solution.py:9
  113.0 43.7 %all-gather.2.cloned.1.call-start = ((), (), s32[]{:S(2)}) async-start(), calls=%async_computation.6 | async-start | bytes 2359296 | tf_op jit(solution)/shard_map/all_gather | solution.py:76
  128.3 292.5 %all-reduce.5.cloned.1.call-start = ((), (), s32[]{:S(2)}) async-start(), calls=%async_computation.8 | async-start | bytes 4194304 | tf_op jit(solution)/shard_map/psum | solution.py:81
  151.6 3.2 copy-start.4
  156.6 4.0 copy-start.2
  156.6 416.2 %all-reduce.3.cloned.1.call-start = ((), (), s32[]{:S(2)}) async-start(), calls=%async_computation.7 | async-start | bytes 2097152 | tf_op jit(solution)/shard_map/psum | solution.py:80
Sparse Core Ops, SparseCore 0:
  12.9 39.6 reduce-scatter.1
  128.4 23.6 all-gather.1
  158.1 262.6 all-reduce.4
  424.7 148.1 all-reduce.2
where the time goes:
time: 583 us
  waiting for transfers between devices  440 us (75%)
  other arithmetic  43.1 us (7%)
  local copies, waits for them, and re-layouts  36.9 us (6%)
  starting transfers between devices  21 us (4%)
  blocking collectives  15.7 us (3%)
  between operations  14.1 us (2%)
  matrix products  11.5 us (2%)
    psum x1, waiting for transfers between devices, on_device(): two_sum = lax.psum(two_sum, ('feat', 'dom'))  259 us
    psum x1, waiting for transfers between devices, on_device(): one_sum = lax.psum(one_sum.astype(jnp.bfloat16), 'dom').astype(jnp.float32)  149 us
    all_to_all x3, waiting for transfers between devices, trade(): lax.all_to_all(buffer, 'dom', split_axis=0, concat_axis=0, tiled=True)  27 us
    scatter-add x2, other arithmetic, gather_back(): jnp.zeros((nodes + sends.size, span), jnp.float32).at[nbrs.reshape(-1)]  26.1 us
    all_to_all x3, starting transfers between devices, trade(): lax.all_to_all(buffer, 'dom', split_axis=0, concat_axis=0, tiled=True)  20.8 us
    all_to_all x1, blocking collectives, trade(): lax.all_to_all(buffer, 'dom', split_axis=0, concat_axis=0, tiled=True)  15.7 us
    mul x4, local copies, waits for them, and re-layouts, gather_back(): terms = (weight[..., None] * grads[:, None, :]).reshape(-1, span)  14 us
  transfers between devices with their start and end apart: 7, of which 6 were waited for; matrix products, arithmetic and copies ran while one was open for 8% of the time, Pallas kernels for 0%

commit v1 on v0

--- a/solution.py
+++ b/solution.py
@@ -78,7 +78,7 @@
         preferred_element_type=jnp.float32,
     )
     one_sum = lax.psum(one_sum.astype(jnp.bfloat16), "dom").astype(jnp.float32)
-    two_sum = lax.psum(two_sum, ("feat", "dom"))
+    two_sum = lax.psum(lax.psum(two_sum, "feat"), "dom")
     scale = 1.0 / math.sqrt(groups * nodes * parts)
     return (out[None], one_sum * scale, two_sum * scale)
 

time: 583 us -> 534 us (0.916)
  waiting for transfers between devices: 440 us -> 390 us
    psum x1 -> x2, waiting for transfers between devices: 259 us -> 180 us  [on_device(): two_sum = lax.psum(lax.psum(two_sum, 'feat'), 'dom')]
    all_gather x1, waiting for transfers between devices: 0.02 us -> 31.2 us  [on_device(): lax.all_gather(d_proj, 'feat', axis=0, tiled=True)]
  transfers between devices with their start and end apart: 7 -> 8, of which waited for: 6 -> 8; matrix products, arithmetic and copies ran while one was open for 8% -> 11% of each run, Pallas kernels for 0% -> 0%
where the time goes in v1:
time: 534 us
  waiting for transfers between devices  390 us (73%)
  other arithmetic  43.8 us (8%)
  local copies, waits for them, and re-layouts  36.8 us (7%)
  starting transfers between devices  21 us (4%)
  blocking collectives  16 us (3%)
  between operations  14.1 us (3%)
  matrix products  11.5 us (2%)
    psum x2, waiting for transfers between devices, on_device(): two_sum = lax.psum(lax.psum(two_sum, 'feat'), 'dom')  180 us
    psum x1, waiting for transfers between devices, on_device(): one_sum = lax.psum(one_sum.astype(jnp.bfloat16), 'dom').astype(jnp.float32)  147 us
    all_gather x1, waiting for transfers between devices, on_device(): lax.all_gather(d_proj, 'feat', axis=0, tiled=True)  31.2 us
    all_to_all x3, waiting for transfers between devices, trade(): lax.all_to_all(buffer, 'dom', split_axis=0, concat_axis=0, tiled=True)  26.6 us
    scatter-add x2, other arithmetic, gather_back(): jnp.zeros((nodes + sends.size, span), jnp.float32).at[nbrs.reshape(-1)]  26.2 us
    all_to_all x3, starting transfers between devices, trade(): lax.all_to_all(buffer, 'dom', split_axis=0, concat_axis=0, tiled=True)  20.8 us
    all_to_all x1, blocking collectives, trade(): lax.all_to_all(buffer, 'dom', split_axis=0, concat_axis=0, tiled=True)  16 us
    mul x4, local copies, waits for them, and re-layouts, gather_back(): terms = (weight[..., None] * grads[:, None, :]).reshape(-1, span)  14 us
  transfers between devices with their start and end apart: 8, of which 8 were waited for; matrix products, arithmetic and copies ran while one was open for 11% of the time, Pallas kernels for 0%

profile of v1, /device:TPU:8, one launch (start us, length us, event | category | flops | bytes accessed | tf_op | source)
XLA Modules:
  0.0 533.6 jit_solution(9362710205576431516)
XLA Ops:
  8.4 4.4 fusion.26
  14.5 2.5 mul.73
  17.0 4.5 mul.74
  21.9 13.1 %scatter_custom_fusion = f32[384,512]{1,0:T(8,128)S(1)} fusion(s32[1280]{0:T(1024)S(1)} %fusion.22, f32[1280,512]{1,0:T(8,128)} %mul.74, f32[1280]{0:T(1024)S(1)} %div.23, f32[]{:T(128)} %constant.9.clone.1), kind=kCustom, calls=%fused_computation.12 | custom fusion | flops 1310720 | bytes 3416068 | tf_op jit(solution)/shard_map/scatter-add | solution.py:36
  35.7 11.3 %all-to-all-start.2 = ((bf16[32,8,512]{2,1,0:T(8,128)(2,1)}), bf16[32,8,512]{2,1,0:T(8,128)(2,1)S(1)}, u32[]{:S(2)}, u32[]{:S(2)}) async-start(bf16[32,8,512]{2,1,0:T(8,128)(2,1)} %fusion.14), calls=%async_computation.3 | async-start | bytes 524288 | tf_op jit(solution)/shard_map/all_to_all | solution.py:9
  47.5 5.2 reduce-scatter.2.cloned.1.call-done
  55.5 4.2 all-to-all-done.2
  59.7 5.7 %all-to-all-start = ((bf16[32,8,512]{2,1,0:T(8,128)(2,1)}), bf16[32,8,512]{2,1,0:T(8,128)(2,1)S(1)}, u32[]{:S(2)}, u32[]{:S(2)}) async-start(bf16[32,8,512]{2,1,0:T(8,128)(2,1)} %bitcast.2), calls=%async_computation.1 | async-start | bytes 524288 | tf_op jit(solution)/shard_map/all_to_all | solution.py:9
  68.1 10.5 %all-to-all-done = bf16[32,8,512]{2,1,0:T(8,128)(2,1)S(1)} async-done(((bf16[32,8,512]{2,1,0:T(8,128)(2,1)}), bf16[32,8,512]{2,1,0:T(8,128)(2,1)S(1)}, u32[]{:S(2)}, u32[]{:S(2)}) %all-to-all-start) | async-done | bytes 262176 | tf_op jit(solution)/shard_map/all_to_all | solution.py:9
  78.7 4.1 gather_fusion.1
  84.9 3.2 multiply_reduce_fusion.1
  90.1 16.0 %all_to_all.20 = bf16[32,8,512]{2,1,0:T(8,128)(2,1)S(1)} all-to-all(bf16[32,8,512]{2,1,0:T(8,128)(2,1)S(1)} %bitcast.50), channel_id=1, replica_groups=mesh['feat'=8,'dom'=32] {'dom'}, dimensions={0} | all-to-all | bytes 524288 | tf_op jit(solution)/shard_map/all_to_all | solution.py:9
  106.1 4.1 gather_fusion.3
  112.3 3.2 multiply_reduce_fusion
  119.8 4.5 mul.80
  124.4 13.2 %scatter_custom_fusion.2 = f32[384,512]{1,0:T(8,128)S(1)} fusion(s32[1280]{0:T(1024)S(1)} %fusion.22, f32[1280,512]{1,0:T(8,128)} %mul.80, f32[1280]{0:T(1024)S(1)} %div.23, f32[]{:T(128)} %constant.9.clone.1), kind=kCustom, calls=%fused_computation.10 | custom fusion | flops 1310720 | bytes 3416068 | tf_op jit(solution)/shard_map/scatter-add | solution.py:36
  138.3 3.9 all-to-all-start.3
  142.2 11.9 %all-to-all-done.3 = bf16[32,8,512]{2,1,0:T(8,128)(2,1)S(1)} async-done(((bf16[32,8,512]{2,1,0:T(8,128)(2,1)}), bf16[32,8,512]{2,1,0:T(8,128)(2,1)S(1)}, u32[]{:S(2)}, u32[]{:S(2)}) %all-to-all-start.3) | async-done | bytes 262176 | tf_op jit(solution)/shard_map/all_to_all | solution.py:9
  157.2 25.7 %all-reduce.6.cloned.1.call-done = f32[1024,512]{1,0:T(8,128)} async-done(((f32[1024,512]{1,0:T(8,128)}), f32[1024,512]{1,0:T(8,128)}) %all-reduce.6.cloned.1.call-update) | async-done | bytes 2097168 | tf_op jit(solution)/shard_map/psum | solution.py:81
  183.0 31.2 %all-gather.2.cloned.1.call-done = bf16[1024,1024]{1,0:T(8,128)(2,1)} async-done(((bf16[128,1024]{1,0:T(8,128)(2,1)}), bf16[1024,1024]{1,0:T(8,128)(2,1)}) %all-gather.2.cloned.1.call-update) | async-done | bytes 2097168 | tf_op jit(solution)/shard_map/all_gather | solution.py:76
  214.2 3.8 fusion.4
  219.0 154.2 %all-reduce.8.cloned.1.call-done = f32[1024,512]{1,0:T(8,128)} async-done(((f32[1024,512]{1,0:T(8,128)}), f32[1024,512]{1,0:T(8,128)}) %all-reduce.8.cloned.1.call-update) | async-done | bytes 2097168 | tf_op jit(solution)/shard_map/psum | solution.py:81
  373.2 3.2 broadcast_multiply_fusion
  376.4 147.3 %all-reduce.4.cloned.1.call-done = bf16[512,1024]{0,1:T(8,128)(2,1)} async-done(((bf16[512,1024]{0,1:T(8,128)(2,1)}), bf16[512,1024]{0,1:T(8,128)(2,1)}) %all-reduce.4.cloned.1.call-update) | async-done | bytes 1048592 | tf_op jit(solution)/shard_map/psum | solution.py:80
  (70 shorter events, 28.5 us)
Async XLA Ops:
  7.2 1.2 copy-start
  7.2 45.5 %reduce-scatter.2.cloned.1.call-start = ((), (), s32[]{:S(2)}) async-start(), calls=%async_computation.5 | async-start | bytes 4718592 | tf_op jit(solution)/shard_map/reduce_scatter | solution.py:48
  12.8 0.7 copy-start.7
  12.8 1.2 copy-start.1
  12.8 1.2 copy-start.4
  17.0 4.5 copy-start.9
  21.6 25.4 %copy-start.8 = (s32[1,32,8]{1,2,0:T(8,128)S(1)}, s32[1,32,8]{1,2,0:T(8,128)}, u32[]{:S(2)}) copy-start(s32[1,32,8]{1,2,0:T(8,128)} %param.12) | copy-start | bytes 3076
  35.7 24.0 %all-to-all-start.2 = ((bf16[32,8,512]{2,1,0:T(8,128)(2,1)}), bf16[32,8,512]{2,1,0:T(8,128)(2,1)S(1)}, u32[]{:S(2)}, u32[]{:S(2)}) async-start(bf16[32,8,512]{2,1,0:T(8,128)(2,1)} %fusion.14), calls=%async_computation.3 | async-start | bytes 524288 | tf_op jit(solution)/shard_map/all_to_all | solution.py:9
  59.7 18.9 %all-to-all-start = ((bf16[32,8,512]{2,1,0:T(8,128)(2,1)}), bf16[32,8,512]{2,1,0:T(8,128)(2,1)S(1)}, u32[]{:S(2)}, u32[]{:S(2)}) async-start(bf16[32,8,512]{2,1,0:T(8,128)(2,1)} %bitcast.2), calls=%async_computation.1 | async-start | bytes 524288 | tf_op jit(solution)/shard_map/all_to_all | solution.py:9
  65.4 117.5 %all-reduce.6.cloned.1.call-start = ((), (), s32[]{:S(2)}) async-start(), calls=%async_computation.8 | async-start | bytes 4194304 | tf_op jit(solution)/shard_map/psum | solution.py:81
  84.9 3.3 copy-start.6
  112.3 3.2 copy-start.5
  124.3 32.0 %copy-start.3 = (bf16[128,512]{1,0:T(8,128)(2,1)S(1)}, bf16[128,512]{1,0:T(8,128)(2,1)}, u32[]{:S(2)}) copy-start(bf16[128,512]{1,0:T(8,128)(2,1)} %get-tuple-element.9) | copy-start | bytes 393220
  138.3 15.9 %all-to-all-start.3 = ((bf16[32,8,512]{2,1,0:T(8,128)(2,1)}), bf16[32,8,512]{2,1,0:T(8,128)(2,1)S(1)}, u32[]{:S(2)}, u32[]{:S(2)}) async-start(bf16[32,8,512]{2,1,0:T(8,128)(2,1)} %fusion.15), calls=%async_computation.4 | async-start | bytes 524288 | tf_op jit(solution)/shard_map/all_to_all | solution.py:9
  142.1 72.0 %all-gather.2.cloned.1.call-start = ((), (), s32[]{:S(2)}) async-start(), calls=%async_computation.6 | async-start | bytes 2359296 | tf_op jit(solution)/shard_map/all_gather | solution.py:76
  157.2 216.1 %all-reduce.8.cloned.1.call-start = ((), (), s32[]{:S(2)}) async-start(), calls=%async_computation.9 | async-start | bytes 4194304 | tf_op jit(solution)/shard_map/psum | solution.py:81
  182.9 35.1 %copy-start.2 = (bf16[1024,512]{1,0:T(8,128)(2,1)S(1)}, bf16[1024,512]{1,0:T(8,128)(2,1)}, u32[]{:S(2)}) copy-start(bf16[1024,512]{1,0:T(8,128)(2,1)} %param.9) | copy-start | bytes 3145732
  182.9 340.7 %all-reduce.4.cloned.1.call-start = ((), (), s32[]{:S(2)}) async-start(), calls=%async_computation.7 | async-start | bytes 2097152 | tf_op jit(solution)/shard_map/psum | solution.py:80
Sparse Core Ops, SparseCore 0:
  12.9 39.6 reduce-scatter.1
  117.5 65.3 all-reduce.5
  185.3 28.7 all-gather.1
  217.5 155.6 all-reduce.7
  377.5 146.1 all-reduce.3
